TPU v7x, 32 devices: a whole 2x2x4 slice. The times are simulated.
32 devices in a mesh: band: 2 (over y), dom: 16 (over z, x, core).
Axes of the slice: x: 2, y: 2, z: 4, core: 2. Of those that a mesh axis runs over, the one named last changes fastest.
Arguments:
- states_in: float32 [128, 16384], P('band', 'dom'), may hold values from -6 to 6
- stiffness: float32 [343, 343], replicated, may hold values from -2 to 2, as said below
- cell_scale: float32 [96], P('dom'), may hold values from 0.5 to 2
- potential: float32 [16384], P('dom'), may hold values from 0 to 2
- inv_mass_sqrt: float32 [16384], P('dom'), may hold values from 0.25 to 1.75
- cell_nodes: int32 [96, 343], P('dom'), may hold values from 0 to 1151, as said below
- shared_nodes: int32 [2048], P('dom'), may hold values from 0 to 1023, as said below
Outputs:
- filtered: float32 [128, 16384], P('band', 'dom')
- margin: float32 [128, 128], P('band')
Inputs may be any that keep to these rules, and one draw needn't show every extreme that they name: `stiffness`: symmetric. `cell_nodes`: in the cells of a subdomain, an entry below 1024 is one of its own nodes and an entry l of 1024 or more stands for entry l - 1024 of the next subdomain's (cyclically) shared_nodes list; every value from 0 to 1151 occurs in the subdomain's cells. `shared_nodes`: the 128 entries of each subdomain are distinct.
All inputs are finite; a program needn't handle non-finite values.
Results may differ from a plain program's by a relative error of at most 0.0001.
Values sent between devices are 32-bit elements; how exact they have to be, the bound alone decides.
A program may use at most 64 MiB of HBM per device.

v0:
```python
import jax
import jax.numpy as jnp
from jax import lax
from jax.sharding import PartitionSpec as P

DEGREE = 3


center_shift = 1.0
half_width = 4.0


def passed_along(x, axis, by):
    peers = lax.axis_size(axis)
    return lax.ppermute(x, axis, [(i, (i + by) % peers) for i in range(peers)])


def per_device(
    states_in, stiffness, cell_scale, potential, inv_mass_sqrt, cell_nodes, shared_nodes
):
    owned = states_in.shape[1]
    shared_count = shared_nodes.shape[0]
    block_rows = states_in.shape[0]

    def operate(vector):
        scaled = vector * inv_mass_sqrt[None, :]
        outgoing = jnp.take(scaled, shared_nodes, axis=1)
        ghosts = passed_along(outgoing, "dom", -1)
        extended = jnp.concatenate([scaled, ghosts], axis=1)
        cellwise = jnp.take(extended, cell_nodes, axis=1)
        product = jnp.einsum(
            "bcj,kj->bck",
            cellwise,
            stiffness,
            precision=lax.Precision.HIGHEST,
            preferred_element_type=jnp.float32,
        )
        product = product * cell_scale[None, :, None]
        summed = (
            jnp.zeros((block_rows, owned + shared_count), jnp.float32)
            .at[:, cell_nodes]
            .add(product)
        )
        returned = passed_along(summed[:, owned:], "dom", 1)
        own_sums = summed[:, :owned].at[:, shared_nodes].add(returned)
        return inv_mass_sqrt[None, :] * own_sums + potential[None, :] * vector

    previous = states_in
    current = (operate(states_in) - center_shift * states_in) / half_width
    for degree_step in range(DEGREE - 1):
        following = 2.0 * (operate(current) - center_shift * current) / half_width - previous
        previous = current
        current = following
    total_nodes = owned * lax.axis_size("dom")
    contract = (((1,), (1,)), ((), ()))
    partial_gram = lax.dot_general(
        current,
        lax.all_gather(current, "band", axis=0, tiled=True),
        contract,
        precision=lax.Precision.HIGHEST,
        preferred_element_type=jnp.float32,
    )
    row_block = partial_gram
    row_block = lax.psum(row_block, "dom")
    return (current, row_block / total_nodes)


def solution(mesh):
    return jax.shard_map(
        per_device,
        mesh=mesh,
        in_specs=(P("band", "dom"), P(), P("dom"), P("dom"), P("dom"), P("dom", None), P("dom")),
        out_specs=(P("band", "dom"), P("band", None)),
        check_vma=False,
    )
```

profile of v0, /device:TPU:0, one launch (start us, length us, event | category | flops | bytes accessed | tf_op | source)
XLA Modules:
  0.0 184.3 jit_solution(14820865741324628735)
XLA Ops:
  0.6 0.7 compare_select_fusion.1
  1.4 0.7 compare_and_fusion.1
  2.0 1.1 copy.34
  3.2 0.9 broadcast_multiply_fusion.2
  4.1 0.6 gather_fusion
  4.8 5.5 %collective-permute-start = (f32[64,128]{0,1:T(8,128)S(1)}, f32[64,128]{0,1:T(8,128)S(1)}, u32[]{:S(2)}, u32[]{:S(2)}) collective-permute-start(f32[64,128]{0,1:T(8,128)S(1)} %select_bitcast_fusion.5), channel_id=1, source_target_pairs={{0,15},{1,0},{2,1},{3,2},{4,3},{5,4},{6,5},{7,6},{8,7},{9,8},{10,9... | collective-permute-start | bytes 98312 | tf_op jit(solution)/shard_map/ppermute | solution.py:15
  10.4 1.8 collective-permute-done
  12.3 3.9 %gather_fusion.1 = f32[2058,64]{1,0:T(8,128)S(1)} fusion(f32[64,1152]{0,1:T(8,128)S(1)} %pad_maximum_fusion, s32[3072]{0:T(1024)S(1)} %pad_clamp_fusion), kind=kCustom, calls=%fused_computation.1.clone | custom fusion | bytes 1061928 | tf_op jit(solution)/shard_map/jit(_take)/gather | solution.py:30
  16.2 0.3 copy.35
  16.6 0.4 reshape.136
  17.1 0.6 copy-done.5
  17.6 1.3 fusion
  18.9 0.3 copy.52
  19.3 1.1 reshape.150
  20.3 14.7 %scatter_custom_fusion = f32[64,1152]{0,1:T(8,128)S(1)} fusion(s32[2058]{0:T(1024)S(1)} %reshape.99, f32[2058,64]{1,0:T(8,128)} %reshape.150, f32[]{:T(128)} %constant.23.clone.1), kind=kCustom, calls=%fused_computation.37 | custom fusion | flops 131712 | bytes 295424 | tf_op jit(solution)/shard_map/scatter-add | solution.py:42
  35.2 6.4 %collective-permute-done.1 = f32[64,128]{0,1:T(8,128)S(1)} collective-permute-done((f32[64,128]{0,1:T(8,128)S(1)}, f32[64,128]{0,1:T(8,128)S(1)}, u32[]{:S(2)}, u32[]{:S(2)}) %collective-permute-start.1) | collective-permute-done | bytes 32800 | tf_op jit(solution)/shard_map/ppermute | solution.py:15
  41.6 1.5 scatter_custom_fusion.1
  43.0 0.5 broadcast_multiply_fusion
  43.5 0.6 gather_fusion.2
  44.2 0.2 collective-permute-start.2
  44.5 1.9 %collective-permute-done.2 = f32[64,128]{0,1:T(8,128)S(1)} collective-permute-done((f32[64,128]{0,1:T(8,128)S(1)}, f32[64,128]{0,1:T(8,128)S(1)}, u32[]{:S(2)}, u32[]{:S(2)}) %collective-permute-start.2) | collective-permute-done | bytes 32800 | tf_op jit(solution)/shard_map/ppermute | solution.py:15
  46.4 5.0 %gather_fusion.3 = f32[2058,64]{1,0:T(8,128)} fusion(f32[64,1152]{0,1:T(8,128)S(1)} %pad_maximum_fusion.1, s32[3072]{0:T(1024)S(1)} %pad_clamp_fusion), kind=kCustom, calls=%fused_computation.4.clone | custom fusion | bytes 1061928 | tf_op jit(solution)/shard_map/jit(_take)/gather | solution.py:30
  51.4 1.6 copy.41
  53.0 0.4 reshape.142
  53.5 1.3 fusion.1
  54.8 0.3 copy.53
  55.1 1.1 reshape.151
  56.2 14.7 %scatter_custom_fusion.2 = f32[64,1152]{0,1:T(8,128)S(1)} fusion(s32[2058]{0:T(1024)S(1)} %reshape.99, f32[2058,64]{1,0:T(8,128)} %reshape.151, f32[]{:T(128)} %constant.23.clone.1), kind=kCustom, calls=%fused_computation.35 | custom fusion | flops 131712 | bytes 295424 | tf_op jit(solution)/shard_map/scatter-add | solution.py:42
  71.0 6.4 %collective-permute-done.3 = f32[64,128]{0,1:T(8,128)S(1)} collective-permute-done((f32[64,128]{0,1:T(8,128)S(1)}, f32[64,128]{0,1:T(8,128)S(1)}, u32[]{:S(2)}, u32[]{:S(2)}) %collective-permute-start.3) | collective-permute-done | bytes 32800 | tf_op jit(solution)/shard_map/ppermute | solution.py:15
  77.4 1.5 scatter_custom_fusion.3
  78.9 0.5 broadcast_multiply_fusion.1
  79.4 0.6 gather_fusion.4
  80.2 1.9 %collective-permute-done.4 = f32[64,128]{0,1:T(8,128)S(1)} collective-permute-done((f32[64,128]{0,1:T(8,128)S(1)}, f32[64,128]{0,1:T(8,128)S(1)}, u32[]{:S(2)}, u32[]{:S(2)}) %collective-permute-start.4) | collective-permute-done | bytes 32800 | tf_op jit(solution)/shard_map/ppermute | solution.py:15
  82.1 5.0 %gather_fusion.5 = f32[2058,64]{1,0:T(8,128)} fusion(f32[64,1152]{0,1:T(8,128)S(1)} %pad_maximum_fusion.2, s32[3072]{0:T(1024)S(1)} %pad_clamp_fusion), kind=kCustom, calls=%fused_computation.5.clone | custom fusion | bytes 1061928 | tf_op jit(solution)/shard_map/jit(_take)/gather | solution.py:30
  87.1 1.6 copy.46
  88.7 0.4 reshape.148
  89.1 2.1 %fusion.2 = f32[6,343,64]{1,2,0:T(8,128)} fusion(f32[64,6,343]{2,1,0:T(8,128)S(1)} %select_bitcast_fusion, f32[343,343]{1,0:T(8,128)S(1)} %copy-done, f32[6]{0:T(128)S(1)} %copy-done.5), kind=kOutput, calls=%fused_computation.17 | convolution fusion | flops 542258304 | bytes 1524316 | tf_op jit(solution)/shard_map/bcj,kj->bck/dot_general | solution.py:31
  91.2 1.4 copy.54
  92.7 1.1 reshape.152
  93.7 14.7 %scatter_custom_fusion.4 = f32[64,1152]{0,1:T(8,128)S(1)} fusion(s32[2058]{0:T(1024)S(1)} %reshape.99, f32[2058,64]{1,0:T(8,128)} %reshape.152, f32[]{:T(128)} %constant.23.clone.1), kind=kCustom, calls=%fused_computation.33 | custom fusion | flops 131712 | bytes 295424 | tf_op jit(solution)/shard_map/scatter-add | solution.py:42
  108.6 6.4 %collective-permute-done.5 = f32[64,128]{0,1:T(8,128)S(1)} collective-permute-done((f32[64,128]{0,1:T(8,128)S(1)}, f32[64,128]{0,1:T(8,128)S(1)}, u32[]{:S(2)}, u32[]{:S(2)}) %collective-permute-start.5) | collective-permute-done | bytes 32800 | tf_op jit(solution)/shard_map/ppermute | solution.py:15
  114.9 1.7 scatter_custom_fusion.5
  116.6 0.5 multiply_subtract_fusion
  117.1 0.2 copy.51
  117.3 7.0 %all_gather.3 = f32[128,1024]{1,0:T(8,128)S(1)} all-gather(f32[64,1024]{1,0:T(8,128)S(1)} %copy.51), channel_id=1, replica_groups=mesh['band'=2,'dom'=16] {'band'}, dimensions={0}, use_global_device_ids=true | all-gather | bytes 786432 | tf_op jit(solution)/shard_map/all_gather | solution.py:58
  124.4 1.0 fusion.21
  125.4 58.3 %psum.7 = f32[64,128]{1,0:T(8,128)S(1)} all-reduce(f32[64,128]{1,0:T(8,128)S(1)} %fusion.21), channel_id=1, replica_groups=mesh['band'=2,'dom'=16] {'dom'}, use_global_device_ids=true, to_apply=%region_6.9 | all-reduce | flops 8192 | bytes 65536 | tf_op jit(solution)/shard_map/psum | solution.py:64
  183.7 0.6 broadcast_multiply_fusion.3
  (37 shorter events, 1.1 us)
Async XLA Ops:
  0.6 16.4 %copy-start = (f32[343,343]{1,0:T(8,128)S(1)}, f32[343,343]{1,0:T(8,128)}, u32[]{:S(2)}) copy-start(f32[343,343]{1,0:T(8,128)} %param.12) | copy-start | bytes 1411792
  2.0 8.3 %copy-start.4 = (s32[6,343]{1,0:T(8,128)S(1)}, s32[6,343]{1,0:T(8,128)}, u32[]{:S(2)}) copy-start(s32[6,343]{1,0:T(8,128)} %param.16) | copy-start | bytes 24700
  4.8 7.4 %collective-permute-start = (f32[64,128]{0,1:T(8,128)S(1)}, f32[64,128]{0,1:T(8,128)S(1)}, u32[]{:S(2)}, u32[]{:S(2)}) collective-permute-start(f32[64,128]{0,1:T(8,128)S(1)} %select_bitcast_fusion.5), channel_id=1, source_target_pairs={{0,15},{1,0},{2,1},{3,2},{4,3},{5,4},{6,5},{7,6},{8,7},{9,8},{10,9... | collective-permute-start | bytes 98312 | tf_op jit(solution)/shard_map/ppermute | solution.py:15
  16.9 0.7 copy-start.5
  19.2 15.9 %copy-start.2 = (f32[1024]{0:T(1024)S(1)}, f32[1024]{0:T(1024)}, u32[]{:S(2)}) copy-start(f32[1024]{0:T(1024)} %param.15) | copy-start | bytes 12292
  20.3 22.7 %copy-start.3 = (f32[1024]{0:T(1024)S(1)}, f32[1024]{0:T(1024)}, u32[]{:S(2)}) copy-start(f32[1024]{0:T(1024)} %param.14) | copy-start | bytes 12292
  35.1 6.5 %collective-permute-start.1 = (f32[64,128]{0,1:T(8,128)S(1)}, f32[64,128]{0,1:T(8,128)S(1)}, u32[]{:S(2)}, u32[]{:S(2)}) collective-permute-start(f32[64,128]{0,1:T(8,128)S(1)} %slice.37), channel_id=1, source_target_pairs={{0,1},{1,2},{2,3},{3,4},{4,5},{5,6},{6,7},{7,8},{8,9},{9,10},{10,1... | collective-permute-start | bytes 98312 | tf_op jit(solution)/shard_map/ppermute | solution.py:15
  44.2 2.1 %collective-permute-start.2 = (f32[64,128]{0,1:T(8,128)S(1)}, f32[64,128]{0,1:T(8,128)S(1)}, u32[]{:S(2)}, u32[]{:S(2)}) collective-permute-start(f32[64,128]{0,1:T(8,128)S(1)} %select_bitcast_fusion.4), channel_id=1, source_target_pairs={{0,15},{1,0},{2,1},{3,2},{4,3},{5,4},{6,5},{7,6},{8,7},{9,8},{10,9... | collective-permute-start | bytes 98312 | tf_op jit(solution)/shard_map/ppermute | solution.py:15
  70.9 6.5 %collective-permute-start.3 = (f32[64,128]{0,1:T(8,128)S(1)}, f32[64,128]{0,1:T(8,128)S(1)}, u32[]{:S(2)}, u32[]{:S(2)}) collective-permute-start(f32[64,128]{0,1:T(8,128)S(1)} %slice.39), channel_id=1, source_target_pairs={{0,1},{1,2},{2,3},{3,4},{4,5},{5,6},{6,7},{7,8},{8,9},{9,10},{10,1... | collective-permute-start | bytes 98312 | tf_op jit(solution)/shard_map/ppermute | solution.py:15
  80.1 2.0 %collective-permute-start.4 = (f32[64,128]{0,1:T(8,128)S(1)}, f32[64,128]{0,1:T(8,128)S(1)}, u32[]{:S(2)}, u32[]{:S(2)}) collective-permute-start(f32[64,128]{0,1:T(8,128)S(1)} %select_bitcast_fusion.3), channel_id=1, source_target_pairs={{0,15},{1,0},{2,1},{3,2},{4,3},{5,4},{6,5},{7,6},{8,7},{9,8},{10,9... | collective-permute-start | bytes 98312 | tf_op jit(solution)/shard_map/ppermute | solution.py:15
  108.5 6.5 %collective-permute-start.5 = (f32[64,128]{0,1:T(8,128)S(1)}, f32[64,128]{0,1:T(8,128)S(1)}, u32[]{:S(2)}, u32[]{:S(2)}) collective-permute-start(f32[64,128]{0,1:T(8,128)S(1)} %slice.41), channel_id=1, source_target_pairs={{0,1},{1,2},{2,3},{3,4},{4,5},{5,6},{6,7},{7,8},{8,9},{9,10},{10,1... | collective-permute-start | bytes 98312 | tf_op jit(solution)/shard_map/ppermute | solution.py:15
  117.3 67.0 %copy-start.1 = (f32[64,1024]{1,0:T(8,128)}, f32[64,1024]{1,0:T(8,128)S(1)}, u32[]{:S(2)}) copy-start(f32[64,1024]{1,0:T(8,128)S(1)} %copy.51) | copy-start | bytes 786436
where the time goes:
time: 185 us; the launch traced here: 184 us
  blocking collectives  65.3 us (35%)
  other arithmetic  53.7 us (29%)
  local copies, waits for them, and re-layouts  27.8 us (15%)
  waiting for transfers between devices  24.7 us (13%)
  starting transfers between devices  5.96 us (3%)
  matrix products  5.69 us (3%)
    psum x1, blocking collectives, per_device(): row_block = lax.psum(row_block, 'dom')  58.3 us
    scatter-add x3, other arithmetic, operate(): summed = jnp.zeros((block_rows, owned + shared_count), jnp.float32).at[:,...  44.2 us
    ppermute x6, waiting for transfers between devices, passed_along(): return lax.ppermute(x, axis, [(i, (i + by) % peers) for i in range(peers)])  24.7 us
    gather x9, local copies, waits for them, and re-layouts, operate(): cellwise = jnp.take(extended, cell_nodes, axis=1)  18.5 us
    all_gather x1, blocking collectives, per_device(): lax.all_gather(current, 'band', axis=0, tiled=True)  7.04 us
    ppermute x6, starting transfers between devices, passed_along(): return lax.ppermute(x, axis, [(i, (i + by) % peers) for i in range(peers)])  5.96 us
    mul x6, local copies, waits for them, and re-layouts, operate(): product = product * cell_scale[None, :, None]  5.25 us
    dot_general x3, matrix products, operate(): jnp.einsum('bcj,kj->bck', cellwise, stiffness, precision=lax.Precision.HI...  4.7 us
  transfers between devices with their start and end apart: 6, of which 6 were waited for; matrix products, arithmetic and copies ran while one was open for 0% of the time, Pallas kernels for 0%

commit v1 on v0

v1 whole, which is shorter than its diff:
```python
import functools

import jax
import jax.numpy as jnp
from jax import lax
from jax.experimental import pallas as pl
from jax.experimental.pallas import tpu as pltpu
from jax.sharding import PartitionSpec as P

DEGREE = 3
CENTER = 1.0
HALF_WIDTH = 4.0
LANES = 128
F32, BF16 = jnp.float32, jnp.bfloat16


def stacked_parts(value):
    high = value.astype(BF16)
    low = (value - high.astype(F32)).astype(BF16)
    return jnp.concatenate([high, low], axis=0)


def folded(value):
    half = value.shape[0] // 2
    return value[:half] + value[half:]


def dot(a, b):
    return jnp.dot(a, b, preferred_element_type=F32)


def dot_nt(a, b):
    return lax.dot_general(a, b, (((1,), (1,)), ((), ())), preferred_element_type=F32)


def one_hot(a, b):
    return jnp.where(a == b, 1.0, 0.0).astype(F32)


def kernel(
    n_band, n_dom, inner,
    x_ref, stiff_ref, scale_ref, pot_ref, mass_ref, cells_ref, shared_ref,
    filt_ref, margin_ref,
    idx, stiff_pad, stiff_hi, stiff_lo, gather, scatter, spread, lead,
    lead_send, lead_recv, ret_send, ret_recv, last_recv, part_send, part_recv,
    uu, yy, zz, block_send, blocks, gram, gram_recv, chunk, chunk_recv, final,
    lead_sem, ret_sem, last_sem, part_sem, block_sem, gram_sem, chunk_sem, final_sem,
):
    rows, owned = x_ref.shape
    cells, npc = cells_ref.shape
    shared = shared_ref.shape[1]
    width = idx.shape[1]
    edge = 2 * shared
    outer = n_dom // inner
    band, dom = lax.axis_index("band"), lax.axis_index("dom")
    after, before = lax.rem(dom + 1, n_dom), lax.rem(dom + n_dom - 1, n_dom)
    place, line = lax.rem(dom, inner), dom // inner

    def turned(value, by, size):
        return lax.rem(value + by, size)

    def at(b, d):
        return {"band": b, "dom": d}

    barrier = pltpu.get_barrier_semaphore()
    greeted = 0
    for k in range(n_band):
        other = turned(band, k, n_band)
        opposite = turned(band, n_band - k, n_band)
        pl.semaphore_signal(barrier, inc=1, device_id=at(other, after))
        pl.semaphore_signal(barrier, inc=1, device_id=at(opposite, before))
        greeted += 2
        if k:
            pl.semaphore_signal(barrier, inc=1, device_id=at(other, dom))
            greeted += 1
    for k in range(1, inner):
        pl.semaphore_signal(
            barrier, inc=1, device_id=at(band, line * inner + turned(place, k, inner)))
        greeted += 1
    for k in range(1, outer):
        pl.semaphore_signal(
            barrier, inc=1, device_id=at(band, turned(line, k, outer) * inner + place))
        greeted += 1

    started = []

    def send(src, dst, sems, slot, device):
        copy = pltpu.make_async_remote_copy(
            src_ref=src, dst_ref=dst, send_sem=sems.at[0, slot], recv_sem=sems.at[1, slot],
            device_id=device, device_id_type=pl.DeviceIdType.MESH)
        copy.start()
        started.append(copy)
        return copy

    mass, pot = mass_ref[...], pot_ref[...]
    shared_row = shared_ref[...]
    lead[0:rows, :] = x_ref[...]
    lead[rows:rows + 8, :] = jnp.concatenate(
        [mass, pot, jnp.zeros((6, owned), F32)], axis=0)
    pick = one_hot(lax.broadcasted_iota(jnp.int32, (owned, shared), 0), shared_row)
    lead_send[...] = jnp.dot(
        lead[...], pick, precision=lax.Precision.HIGHEST, preferred_element_type=F32)
    pl.semaphore_wait(barrier, greeted)
    lead_copy = send(lead_send, lead_recv, lead_sem, 0, at(band, before))

    idx[...] = jnp.full(idx.shape, -1.0, F32)
    idx[0:cells, 0:npc] = cells_ref[...].astype(F32)
    stiff_pad[...] = jnp.zeros(stiff_pad.shape, F32)
    stiff_pad[0:npc, 0:npc] = stiff_ref[...]
    high = stiff_pad[...].astype(BF16)
    stiff_hi[...] = high
    stiff_lo[...] = (stiff_pad[...] - high.astype(F32)).astype(BF16)
    shared_f = shared_row.astype(F32)
    shared_col = jnp.broadcast_to(shared_f, (LANES, shared)).T
    for k in range(owned // LANES):
        lane = lax.broadcasted_iota(jnp.int32, (shared, LANES), 1) + k * LANES
        spread[:, k * LANES:(k + 1) * LANES] = one_hot(shared_col, lane.astype(F32)).astype(BF16)
    local = owned + shared
    node = lax.broadcasted_iota(jnp.int32, (LANES, width), 0).astype(F32)
    lane = lax.broadcasted_iota(jnp.int32, (width, LANES), 1).astype(F32)
    shared_wide = jnp.concatenate([shared_col] * (width // LANES), axis=1)
    for c in range(cells):
        slot_row = jnp.broadcast_to(idx[c:c + 1, :], (LANES, width))
        slot_col = slot_row.T
        span = slice(c * width, (c + 1) * width)
        for k in range(local // LANES):
            tile = slice(k * LANES, (k + 1) * LANES)
            gather[c, tile, :] = one_hot(node + float(k * LANES), slot_row).astype(BF16)
            scatter[span, tile] = one_hot(lane + float(k * LANES), slot_col).astype(BF16)
        gather[c, local:, :] = one_hot(shared_wide, slot_row).astype(BF16)
        scatter[span, local:] = one_hot(shared_f, slot_col).astype(BF16)

    mass_shared, pot_shared = lead_send[rows:rows + 1, :], lead_send[rows + 1:rows + 2, :]
    partial = x_ref[...]
    current_shared = lead_send[0:rows, :]
    previous, previous_shared = None, None
    returned = None
    for t in range(DEGREE):
        last = t == DEGREE - 1
        factor = (1.0 if t == 0 else 2.0) / HALF_WIDTH
        uu[...] = stacked_parts(mass * partial)
        for c in range(cells):
            yy[c] = dot(uu[...], gather[c, 0:owned, :])
        if t == 0:
            lead_copy.wait_recv()
            mass_ghost = lead_recv[rows:rows + 1, :]
            ghost = lead_recv[0:rows, :]
            fix = None
            outside = stacked_parts(
                jnp.concatenate([mass_ghost * ghost, jnp.zeros_like(ghost)], axis=1))
        else:
            ret_copy.wait_recv()
            part_copy.wait_recv()
            fix = earlier * mass_shared * ret_recv[t - 1]
            ghost = part_recv[t - 1] + earlier * mass_ghost * returned
            current_shared = part + fix
            outside = stacked_parts(
                jnp.concatenate([mass_ghost * ghost, mass_shared * fix], axis=1))
        for c in range(cells):
            y = stacked_parts(folded(yy[c] + dot(outside, gather[c, owned:, :])))
            z = folded(dot(y, stiff_hi[...])) + dot(y[0:rows], stiff_lo[...])
            zz[:, c * width:(c + 1) * width] = stacked_parts(z * scale_ref[c])
        border = folded(dot(zz[...], scatter[:, owned:]))
        returned = border[:, 0:shared]
        ret_send[t] = returned
        if last:
            last_copies = [
                send(ret_send.at[t], last_recv.at[band], last_sem, k,
                     at(turned(band, k, n_band), after))
                for k in range(n_band)]
        else:
            ret_copy = send(ret_send.at[t], ret_recv.at[t], ret_sem, t, at(band, after))
            part = factor * (
                mass_shared * border[:, shared:] + (pot_shared - CENTER) * current_shared)
            if t:
                part = part - previous_shared
            part_send[t] = part
            part_copy = send(part_send.at[t], part_recv.at[t], part_sem, t, at(band, before))
        current = partial
        if t:
            current = current + folded(dot(stacked_parts(fix), spread[...]))
        sums = folded(dot(zz[...], scatter[:, 0:owned]))
        partial = factor * (mass * sums + (pot - CENTER) * current)
        if t:
            partial = partial - previous
        previous, previous_shared = current, current_shared
        earlier = factor

    block_send[...] = partial
    blocks[band] = partial
    block_copies = [
        send(block_send, blocks.at[band], block_sem, k - 1, at(turned(band, k, n_band), dom))
        for k in range(1, n_band)]
    for copy in last_copies:
        copy.wait_recv()
    for copy in block_copies:
        copy.wait_recv()
    for b in range(n_band):
        fix = stacked_parts(earlier * mass_shared * last_recv[b])
        blocks[b] = blocks[b] + folded(dot(fix, spread[...]))
    filtered = blocks[band]
    filt_ref[...] = filtered
    mine = stacked_parts(filtered)
    depth = rows // inner
    pieces = []
    for b in range(n_band):
        theirs = stacked_parts(blocks[b])
        pieces.append(folded(dot_nt(mine, theirs[0:rows])) + dot_nt(mine[0:rows], theirs[rows:]))
    product = jnp.concatenate(pieces, axis=1) * (1.0 / (owned * n_dom))
    for k in range(inner):
        gram[k] = product[k * depth:(k + 1) * depth]
    copies = []
    for k in range(1, inner):
        to = turned(place, k, inner)
        copies.append(send(
            gram.at[to], gram_recv.at[place], gram_sem, k - 1, at(band, line * inner + to)))
    gram_recv[place] = gram[place]
    for copy in copies:
        copy.wait_recv()
    total = gram_recv[0]
    for k in range(1, inner):
        total = total + gram_recv[k]
    chunk[...] = total
    copies = [
        send(chunk, chunk_recv.at[line], chunk_sem, k - 1,
             at(band, turned(line, k, outer) * inner + place))
        for k in range(1, outer)]
    chunk_recv[line] = total
    for copy in copies:
        copy.wait_recv()
    total = chunk_recv[0]
    for k in range(1, outer):
        total = total + chunk_recv[k]
    gram_out = final.at[place]
    gram_out[...] = total
    copies = [
        send(final.at[place], final.at[place], final_sem, k - 1,
             at(band, line * inner + turned(place, k, inner)))
        for k in range(1, inner)]
    for copy in copies:
        copy.wait_recv()
    for k in range(inner):
        margin_ref[k * depth:(k + 1) * depth, :] = final[k]
    for copy in started:
        copy.wait_send()


def rounded_up(value):
    return -(-value // LANES) * LANES


def per_device(
    n_band, n_dom,
    states_in, stiffness, cell_scale, potential, inv_mass_sqrt, cell_nodes, shared_nodes
):
    rows, owned = states_in.shape
    cells, npc = cell_nodes.shape
    shared = shared_nodes.shape[0]
    width = rounded_up(npc)
    nodes = owned + 2 * shared
    states = n_band * rows
    inner = 1
    while inner * inner * 4 <= n_dom:
        inner *= 2
    outer = n_dom // inner
    depth = rows // inner
    pairs = lambda count: pltpu.SemaphoreType.DMA((2, count))
    vmem = pltpu.VMEM
    in_vmem = pl.BlockSpec(memory_space=pltpu.VMEM)
    return pl.pallas_call(
        functools.partial(kernel, n_band, n_dom, inner),
        out_shape=(
            jax.ShapeDtypeStruct((rows, owned), F32),
            jax.ShapeDtypeStruct((rows, states), F32),
        ),
        in_specs=[in_vmem, in_vmem, pl.BlockSpec(memory_space=pltpu.SMEM)] + [in_vmem] * 4,
        out_specs=(in_vmem, in_vmem),
        scratch_shapes=[
            vmem((-(-cells // 8) * 8, width), F32),
            vmem((width, width), F32),
            vmem((width, width), BF16),
            vmem((width, width), BF16),
            vmem((cells, nodes, width), BF16),
            vmem((cells * width, nodes), BF16),
            vmem((shared, owned), BF16),
            vmem((rows + 8, owned), F32),
            vmem((rows + 8, shared), F32),
            vmem((rows + 8, shared), F32),
            vmem((DEGREE, rows, shared), F32),
            vmem((DEGREE - 1, rows, shared), F32),
            vmem((n_band, rows, shared), F32),
            vmem((DEGREE - 1, rows, shared), F32),
            vmem((DEGREE - 1, rows, shared), F32),
            vmem((2 * rows, owned), BF16),
            vmem((cells, 2 * rows, width), F32),
            vmem((2 * rows, cells * width), BF16),
            vmem((rows, owned), F32),
            vmem((n_band, rows, owned), F32),
            vmem((inner, depth, states), F32),
            vmem((inner, depth, states), F32),
            vmem((depth, states), F32),
            vmem((outer, depth, states), F32),
            vmem((inner, depth, states), F32),
            pairs(1),
            pairs(DEGREE - 1),
            pairs(n_band),
            pairs(DEGREE - 1),
            pairs(max(n_band - 1, 1)),
            pairs(max(inner - 1, 1)),
            pairs(max(outer - 1, 1)),
            pairs(max(inner - 1, 1)),
        ],
        compiler_params=pltpu.CompilerParams(collective_id=0, has_side_effects=True),
    )(
        states_in, stiffness, cell_scale, potential[None, :], inv_mass_sqrt[None, :],
        cell_nodes, shared_nodes[None, :],
    )


def solution(mesh):
    n_band, n_dom = mesh.shape["band"], mesh.shape["dom"]
    return jax.shard_map(
        functools.partial(per_device, n_band, n_dom),
        mesh=mesh,
        in_specs=(P("band", "dom"), P(), P("dom"), P("dom"), P("dom"), P("dom", None), P("dom")),
        out_specs=(P("band", "dom"), P("band", None)),
        check_vma=False,
    )
```

time: 185 us -> 44.3 us (0.24)
  blocking collectives: 65.3 us -> 0 us
  other arithmetic: 53.7 us -> 0 us
  Pallas kernels: 0 us -> 41.1 us
  local copies, waits for them, and re-layouts: 27.8 us -> 2.3 us
  waiting for transfers between devices: 24.7 us -> 0 us
  starting transfers between devices: 5.96 us -> 0 us
  matrix products: 5.69 us -> 0 us
    psum x1 -> x0, blocking collectives: 58.3 us -> none  [per_device(): row_block = lax.psum(row_block, 'dom')]
    scatter-add x6 -> x0, other arithmetic: 48.7 us -> none  [the longest x3 44.2 us: operate(): summed = jnp.zeros((block_rows, owned + shared_count), jnp.float32).at[:,...]
    pallas_call x0 -> x1, Pallas kernels: none -> 41.1 us  [per_device(): pl.pallas_call(functools.partial(kernel, n_band, n_dom, inner), out_shape...]
    ppermute x6 -> x0, waiting for transfers between devices: 24.7 us -> none  [passed_along(): return lax.ppermute(x, axis, [(i, (i + by) % peers) for i in range(peers)])]
    gather x12 -> x0, local copies, waits for them, and re-layouts: 20.5 us -> none  [the longest x9 18.5 us: operate(): cellwise = jnp.take(extended, cell_nodes, axis=1)]
    all_gather x1 -> x0, blocking collectives: 7.04 us -> none  [per_device(): lax.all_gather(current, 'band', axis=0, tiled=True)]
    ppermute x6 -> x0, starting transfers between devices: 5.96 us -> none  [passed_along(): return lax.ppermute(x, axis, [(i, (i + by) % peers) for i in range(peers)])]
    dot_general x4 -> x0, matrix products: 5.69 us -> none  [the longest x3 4.7 us: operate(): jnp.einsum('bcj,kj->bck', cellwise, stiffness, precision=lax.Precision.HI...]
  transfers between devices with their start and end apart: 6 -> 0, of which waited for: 6 -> 0; matrix products, arithmetic and copies ran while one was open for 0% -> 0% of each run, Pallas kernels for 0% -> 0%
where the time goes in v1:
time: 44.3 us; the launch traced here: 44.1 us
  Pallas kernels  41.1 us (93%)
  local copies, waits for them, and re-layouts  2.3 us (5%)
  between operations  0.65 us (1%)
    pallas_call x1, Pallas kernels, per_device(): pl.pallas_call(functools.partial(kernel, n_band, n_dom, inner), out_shape...  41.1 us
    unnamed x4, local copies, waits for them, and re-layouts  2.3 us

profile of v1, /device:TPU:0, one launch (start us, length us, event | category | flops | bytes accessed | tf_op | source)
XLA Modules:
  0.0 44.1 jit_solution(4247709908928075538)
XLA Ops:
  0.6 41.1 %shard_map.86 = (f32[64,1024]{1,0:T(8,128)}, f32[64,128]{1,0:T(8,128)}) custom-call(f32[64,1024]{1,0:T(8,128)} %x_ref.1, f32[343,343]{1,0:T(8,128)} %stiff_ref.1, f32[6]{0:T(128)} %scale_ref.1, f32[1,1024]{1,0:T(1,128)} %bitcast.3, f32[1,1024]{1,0:T(1,128)} %bitcast.4, s32[6,343]{1,0:T(8,128)} %cells_ref.1, s32[1,128]{1,0:T(1,128)} %bitcast.5), custom_call_target="tpu_custom_call" | custom-call | tf_op jit(solution)/shard_map/pallas_call | solution.py:270
  41.8 0.0 copy-start
  41.8 1.7 %copy.11 = f32[64,1024]{1,0:T(8,128)} copy(f32[64,1024]{1,0:T(8,128)} %get-tuple-element.4) | data formatting | bytes 524288
  43.5 0.0 copy-done
  43.5 0.6 %copy.12 = f32[64,128]{1,0:T(8,128)} copy(f32[64,128]{1,0:T(8,128)S(1)} %copy-done) | data formatting | bytes 65536
Async XLA Ops:
  41.8 1.7 %copy-start = (f32[64,128]{1,0:T(8,128)S(1)}, f32[64,128]{1,0:T(8,128)}, u32[]{:S(2)}) copy-start(f32[64,128]{1,0:T(8,128)} %get-tuple-element.5) | copy-start | bytes 98308

commit v2 on v1

--- a/solution.py
+++ b/solution.py
@@ -39,8 +39,9 @@
 
 def kernel(
     n_band, n_dom, inner,
-    x_ref, stiff_ref, scale_ref, pot_ref, mass_ref, cells_ref, shared_ref,
+    x_hbm, stiff_hbm, scale_hbm, pot_hbm, mass_hbm, cells_hbm, shared_hbm,
     filt_ref, margin_ref,
+    x_ref, stiff_ref, scale_ref, pot_ref, mass_ref, cells_ref, shared_ref, load_sem,
     idx, stiff_pad, stiff_hi, stiff_lo, gather, scatter, spread, lead,
     lead_send, lead_recv, ret_send, ret_recv, last_recv, part_send, part_recv,
     uu, yy, zz, block_send, blocks, gram, gram_recv, chunk, chunk_recv, final,
@@ -62,6 +63,11 @@
     def at(b, d):
         return {"band": b, "dom": d}
 
+    pairs = (
+        (shared_hbm, shared_ref), (mass_hbm, mass_ref), (pot_hbm, pot_ref), (x_hbm, x_ref),
+        (cells_hbm, cells_ref), (stiff_hbm, stiff_ref), (scale_hbm, scale_ref))
+    loads = [pltpu.make_async_copy(src, dst, load_sem.at[k]) for k, (src, dst) in enumerate(pairs)]
+    first_loads, later_loads = loads[:4], loads[4:]
     barrier = pltpu.get_barrier_semaphore()
     greeted = 0
     for k in range(n_band):
@@ -82,6 +88,8 @@
             barrier, inc=1, device_id=at(band, turned(line, k, outer) * inner + place))
         greeted += 1
 
+    for load in loads:
+        load.start()
     started = []
 
     def send(src, dst, sems, slot, device):
@@ -92,6 +100,8 @@
         started.append(copy)
         return copy
 
+    for load in first_loads:
+        load.wait()
     mass, pot = mass_ref[...], pot_ref[...]
     shared_row = shared_ref[...]
     lead[0:rows, :] = x_ref[...]
@@ -103,6 +113,8 @@
     pl.semaphore_wait(barrier, greeted)
     lead_copy = send(lead_send, lead_recv, lead_sem, 0, at(band, before))
 
+    for load in later_loads:
+        load.wait()
     idx[...] = jnp.full(idx.shape, -1.0, F32)
     idx[0:cells, 0:npc] = cells_ref[...].astype(F32)
     stiff_pad[...] = jnp.zeros(stiff_pad.shape, F32)
@@ -273,9 +285,17 @@
             jax.ShapeDtypeStruct((rows, owned), F32),
             jax.ShapeDtypeStruct((rows, states), F32),
         ),
-        in_specs=[in_vmem, in_vmem, pl.BlockSpec(memory_space=pltpu.SMEM)] + [in_vmem] * 4,
+        in_specs=[pl.BlockSpec(memory_space=pltpu.HBM)] * 7,
         out_specs=(in_vmem, in_vmem),
         scratch_shapes=[
+            vmem((rows, owned), F32),
+            vmem((npc, npc), F32),
+            pltpu.SMEM((cells,), F32),
+            vmem((1, owned), F32),
+            vmem((1, owned), F32),
+            vmem((cells, npc), jnp.int32),
+            vmem((1, shared), jnp.int32),
+            pltpu.SemaphoreType.DMA((7,)),
             vmem((-(-cells // 8) * 8, width), F32),
             vmem((width, width), F32),
             vmem((width, width), BF16),
@@ -310,11 +330,11 @@
             pairs(max(outer - 1, 1)),
             pairs(max(inner - 1, 1)),
         ],
-        compiler_params=pltpu.CompilerParams(collective_id=0, has_side_effects=True),
-    )(
+        compiler_params=pltpu.CompilerParams(collective_id=0, has_side_effects=True, vmem_limit_bytes=28 << 20),
+    )(*[pltpu.with_memory_space_constraint(value, pltpu.HBM) for value in (
         states_in, stiffness, cell_scale, potential[None, :], inv_mass_sqrt[None, :],
         cell_nodes, shared_nodes[None, :],
-    )
+    )])
 
 
 def solution(mesh):

time: 44.3 us -> 41.5 us (0.937)
  Pallas kernels: 41.1 us -> 39.4 us
  local copies, waits for them, and re-layouts: 2.3 us -> 1.32 us
    pallas_call x1, Pallas kernels: 41.1 us -> 39.4 us  [per_device(): pl.pallas_call(functools.partial(kernel, n_band, n_dom, inner), out_shape...]
    unnamed x4 -> x2, local copies, waits for them, and re-layouts: 2.3 us -> 1.32 us
where the time goes in v2:
time: 41.5 us; the launch traced here: 41.4 us
  Pallas kernels  39.4 us (95%)
  local copies, waits for them, and re-layouts  1.32 us (3%)
  between operations  0.64 us (2%)
    pallas_call x1, Pallas kernels, per_device(): pl.pallas_call(functools.partial(kernel, n_band, n_dom, inner), out_shape...  39.4 us
    unnamed x2, local copies, waits for them, and re-layouts  1.32 us

profile of v2, /device:TPU:0, one launch (start us, length us, event | category | flops | bytes accessed | tf_op | source)
XLA Modules:
  0.0 41.4 jit_solution(4635585257971242709)
XLA Ops:
  0.6 39.4 %shard_map.86 = (f32[64,1024]{1,0:T(8,128)S(1)}, f32[64,128]{1,0:T(8,128)S(1)}) custom-call(f32[64,1024]{1,0:T(8,128)} %x_hbm.1, f32[343,343]{1,0:T(8,128)} %stiff_hbm.1, f32[6]{0:T(128)} %scale_hbm.1, f32[1,1024]{1,0:T(1,128)} %bitcast.3, f32[1,1024]{1,0:T(1,128)} %bitcast.4, s32[6,343]{1,0:T(8,128)} %cells_hbm.1, s32[1,128]{1,0:T(1,128)} %bitcast.5), custom_call_target="tpu_custom_call" | custom-call | tf_op jit(solution)/shard_map/pallas_call | solution.py:282
  40.1 0.7 %copy.11 = f32[64,1024]{1,0:T(8,128)} copy(f32[64,1024]{1,0:T(8,128)S(1)} %get-tuple-element.4) | data formatting | bytes 524288
  40.8 0.6 %copy.12 = f32[64,128]{1,0:T(8,128)} copy(f32[64,128]{1,0:T(8,128)S(1)} %get-tuple-element.5) | data formatting | bytes 65536
